TPU v7x, 32 devices: a whole 2x2x4 slice. The times are simulated.
32 devices in a mesh: groups: 2 (over y), shard: 4 (over z), section: 2 (over x), halo: 2 (over core).
Axes of the slice: x: 2, y: 2, z: 4, core: 2. Of those that a mesh axis runs over, the one named last changes fastest.
Arguments:
- features: bfloat16 [4, 4, 16, 64, 320], P(('groups', 'section'), 'shard', 'halo'), parts along dimension 0, may hold values from -6 to 6
- timesteps: int32 [4, 2], P(('groups', 'section')), parts along dimension 0, may hold values from 0 to 999
- conv_first: bfloat16 [2, 3, 3, 320, 320], P('section'), may hold values from -0.109375 to 0.109375
- conv_second: bfloat16 [2, 3, 3, 320, 320], P('section'), may hold values from -0.109375 to 0.109375
- time_weight: bfloat16 [2, 320, 320], P('section'), may hold values from -0.3125 to 0.3125
- qkv_weight: bfloat16 [2, 320, 960], P('section'), may hold values from -7 to 7
- attn_out: bfloat16 [2, 320, 320], P('section'), may hold values from -0.3125 to 0.3125
- geglu_in: bfloat16 [2, 320, 2560], P('section'), may hold values from -0.3125 to 0.3125
- geglu_out: bfloat16 [2, 1280, 320], P('section'), may hold values from -0.15625 to 0.15625
Outputs:
- result: bfloat16 [4, 4, 16, 64, 320], P(('groups', 'section'), 'shard', 'halo'), parts along dimension 0
There are 2 independent parts, one for each index of `groups`. A program takes and returns all parts, laid end to end along the dimension named above; an argument that names none is the same for every part. Nothing has to cross between parts.
All inputs are finite; a program needn't handle non-finite values.
Results may differ from a plain program's by a relative error of at most 0.02.
Values may be sent and summed in bfloat16 or wider, within the bound.
A program may use at most 64 MiB of HBM per device.

v0:
```python
import functools
import math

import jax
import jax.numpy as jnp
from jax import lax
from jax.experimental import pallas as pl
from jax.experimental.pallas import tpu as pltpu
from jax.sharding import PartitionSpec as P

HEAD_DIM = 64
GROUPS = 32
STEPS = 2
MESH = pl.DeviceIdType.MESH
F32 = jnp.float32
BF16 = jnp.bfloat16
BLK = 64
PAD = 8


def matmul(a, b):
    return jnp.dot(a, b, preferred_element_type=F32)


def silu(u):
    return u * (1.0 / (1.0 + jnp.exp(-u)))


def kernel(dims, stamps, feat, cf_h, cs_h, tw_h, qkv_h, ao_h, gi_h, go_h, out, *scratch):
    (rows, width, chans, inner, nsh, nsec) = dims
    (F, H, G, A, S, PB, O, stat_tx, stat_rx, edge_x, edge_h, emb, gmask, hmask, hmask_t,
     N, Q, K, V, PH, PL, OB, S2, ACT,
     cf, cs, tw, qkv, ao, gi, go,
     w_sem, x_sem, halo_send, halo_recv, in_send, in_recv, out_send, out_recv, own_sem) = scratch
    tokens = rows * width
    part = tokens // nsh
    rim = (rows + 2) * width
    me = lax.axis_index("shard")
    sec = lax.axis_index("section")
    side = lax.axis_index("halo")
    nxt = lax.rem(sec + 1, nsec)

    loads = [
        pltpu.make_async_copy(src, dst, w_sem.at[i])
        for i, (src, dst) in enumerate(
            ((cf_h, cf), (cs_h, cs), (tw_h, tw), (qkv_h, qkv), (ao_h, ao), (gi_h, gi), (go_h, go))
        )
    ]
    for load in loads:
        load.start()

    def at(shard, section):
        return {"shard": shard, "section": section}

    barrier = pltpu.get_barrier_semaphore()
    peers = [{"halo": 1 - side}]
    for d in range(1, nsh):
        peers.append(at(lax.rem(me + d, nsh), sec))
    for e in sorted({1 % nsec, (nsec - 1) % nsec} - {0}):
        for d in range(nsh):
            peers.append(at(lax.rem(me + d, nsh), lax.rem(sec + e, nsec)))
    for peer in peers:
        pl.semaphore_signal(barrier, inc=1, device_id=peer, device_id_type=MESH)
    pl.semaphore_wait(barrier, len(peers))

    shift = pltpu.make_async_remote_copy(
        src_ref=feat, dst_ref=F.at[0], send_sem=x_sem.at[0], recv_sem=x_sem.at[1],
        device_id={"section": nxt}, device_id_type=MESH,
    )
    shift.start()

    per = chans // GROUPS
    ci = lax.broadcasted_iota(jnp.int32, (chans, chans), 0)
    cj = lax.broadcasted_iota(jnp.int32, (chans, chans), 1)
    gmask[...] = jnp.where(ci - lax.rem(ci, per) == cj - lax.rem(cj, per), 1.0, 0.0).astype(F32)
    lanes = hmask.shape[1]
    hi_ = lax.broadcasted_iota(jnp.int32, (chans, lanes), 0)
    hj_ = lax.broadcasted_iota(jnp.int32, (chans, lanes), 1)
    hmask[...] = jnp.where(hi_ - lax.rem(hi_, HEAD_DIM) == hj_ * HEAD_DIM, HEAD_DIM ** (-0.5), 0.0).astype(BF16)
    ti_ = lax.broadcasted_iota(jnp.int32, (lanes, chans), 0)
    tj_ = lax.broadcasted_iota(jnp.int32, (lanes, chans), 1)
    hmask_t[...] = jnp.where(tj_ - lax.rem(tj_, HEAD_DIM) == ti_ * HEAD_DIM, 1.0, 0.0).astype(BF16)
    stat_tx[...] = jnp.zeros_like(stat_tx)
    zeros_rim = jnp.zeros((width, chans), F32)
    G[pl.ds(0, PAD), :] = jnp.zeros((PAD, chans), F32)
    G[pl.ds(PAD + rim, PAD), :] = jnp.zeros((PAD, chans), F32)
    G[pl.ds(PAD, width), :] = zeros_rim
    G[pl.ds(PAD + rim - width, width), :] = zeros_rim

    loads[2].wait()
    half = chans // 2
    lane = lax.broadcasted_iota(jnp.int32, (16, chans), 1)
    k_of = jnp.where(lane < half, lane, lane - half).astype(F32)
    frequency = jnp.exp(-math.log(10000.0) * k_of / half)
    for n in range(STEPS):
        angles = stamps[0, n].astype(F32) * frequency
        wave = jnp.where(lane < half, jnp.cos(angles), jnp.sin(angles))
        emb[n] = matmul(silu(wave).astype(BF16), tw[...])

    edge_at = pl.multiple_of((1 - side) * (tokens - width), 16)
    rim_at = pl.multiple_of(PAD + (1 - side) * (rim - width), 8)
    count = float(rows * 2 * width * per)

    def swap(slot, edge_src, edge_dst):
        copies = [
            pltpu.make_async_remote_copy(
                src_ref=src, dst_ref=dst, send_sem=halo_send.at[slot, i], recv_sem=halo_recv.at[slot, i],
                device_id={"halo": 1 - side}, device_id_type=MESH,
            )
            for i, (src, dst) in enumerate(
                ((edge_src, edge_dst), (stat_tx.at[slot], stat_rx.at[slot]))
            )
        ]
        return copies

    def totals(load, slot):
        def one(i, carry):
            s1, s2 = carry
            v = load(pl.ds(pl.multiple_of(i * BLK, BLK), BLK))
            return (s1 + jnp.sum(v.reshape(BLK // 8, 8, chans), axis=0),
                    s2 + jnp.sum((v * v).reshape(BLK // 8, 8, chans), axis=0))
        z = jnp.zeros((8, chans), F32)
        s1, s2 = lax.fori_loop(0, tokens // BLK, one, (z, z))
        stat_tx[slot, 0:1, :] = jnp.sum(s1, axis=0, keepdims=True)
        stat_tx[slot, 1:2, :] = jnp.sum(s2, axis=0, keepdims=True)

    def moments(slot):
        both = stat_tx[slot] + stat_rx[slot]
        summed = jnp.dot(both, gmask[...], preferred_element_type=F32, precision=lax.Precision.HIGHEST)
        average = summed[0:1, :] / count
        second = summed[1:2, :] / count
        return average, lax.rsqrt(second - average * average + 1e-05)

    def activate(load, load_edge, slot):
        average, inverse = moments(slot)

        def one(i, c):
            at_ = pl.multiple_of(i * BLK, BLK)
            G[pl.ds(PAD + width + at_, BLK), :] = silu((load(pl.ds(at_, BLK)) - average) * inverse)
            return c
        lax.fori_loop(0, tokens // BLK, one, 0)
        G[pl.ds(rim_at, width), :] = silu((load_edge() - average) * inverse)
        col = lax.rem(lax.broadcasted_iota(jnp.int32, (width, chans), 0), width)

        def two(i, c):
            at_ = pl.multiple_of(i * width, width)
            window = G[pl.ds(at_, width + 2 * PAD), :]
            left = window[PAD - 1 : PAD - 1 + width]
            mid = window[PAD : PAD + width]
            right = window[PAD + 1 : PAD + 1 + width]
            dst = pl.ds(at_, width)
            A[dst, 0:chans] = jnp.where(col == 0, 0.0, left).astype(BF16)
            A[dst, chans : 2 * chans] = mid.astype(BF16)
            A[dst, 2 * chans :] = jnp.where(col == width - 1, 0.0, right).astype(BF16)
            return c
        lax.fori_loop(0, rows + 2, two, 0)

    def conv(weights):
        total = matmul(A[pl.ds(0, tokens), :], weights[0])
        total += matmul(A[pl.ds(width, tokens), :], weights[1])
        total += matmul(A[pl.ds(2 * width, tokens), :], weights[2])
        return total

    def normalise(src):
        def one(i, c):
            at_ = pl.ds(pl.multiple_of(i * BLK, BLK), BLK)
            v = src(at_)
            centred = v - jnp.mean(v, axis=-1, keepdims=True)
            spread = jnp.mean(centred * centred, axis=-1, keepdims=True)
            N[at_, :] = (centred * lax.rsqrt(spread + 1e-05)).astype(BF16)
            return c
        lax.fori_loop(0, tokens // BLK, one, 0)

    for n in range(STEPS):
        if n == 0:
            shift.wait()
        field = F.at[n]

        def load_x(s, field=field):
            return field[s, :].astype(F32)

        swaps = swap(2 * n, field.at[pl.ds(edge_at, width)], edge_x.at[n])
        swaps[0].start()
        totals(load_x, 2 * n)
        swaps[1].start()
        for s in swaps:
            s.wait()
        activate(load_x, lambda: edge_x[n].astype(F32), 2 * n)
        if n == 0:
            loads[0].wait()
        H[n] = conv(cf) + emb[n, 0:1, :]

        def load_h(s):
            return H[n, s, :]
        swaps = swap(2 * n + 1, H.at[n, pl.ds(edge_at, width)], edge_h.at[n])
        swaps[0].start()
        totals(load_h, 2 * n + 1)
        swaps[1].start()
        for s in swaps:
            s.wait()
        activate(load_h, lambda: edge_h[n], 2 * n + 1)
        if n == 0:
            loads[1].wait()
        S[n] = (conv(cs) + field[...].astype(F32)).astype(BF16).reshape(nsh, part, chans)

        copies = []
        for d in range(1, nsh):
            to = lax.rem(me + d, nsh)
            copies.append(pltpu.make_async_remote_copy(
                src_ref=S.at[n, to], dst_ref=PB.at[n, me],
                send_sem=in_send.at[n, d], recv_sem=in_recv.at[n, d],
                device_id={"shard": to}, device_id_type=MESH,
            ))
            copies[-1].start()
        PB[n, me] = S[n, me]
        for c in copies:
            c.wait()

        if n == 0:
            for i in (3, 4, 5, 6):
                loads[i].wait()
        stream = PB.at[n]

        def load_p(s):
            return stream.reshape(tokens, chans)[s, :].astype(F32)
        normalise(load_p)
        proj = matmul(N[...], qkv[...]).astype(BF16)
        Q[...] = proj[:, :chans].astype(F32)
        K[...] = proj[:, chans : 2 * chans].astype(F32)
        V[...] = proj[:, 2 * chans :].astype(F32)

        def frame(f, c):
            q = Q[pl.ds(pl.multiple_of(f * part, 16), part), :]
            for g in range(nsh):
                prod = q * K[g * part : (g + 1) * part, :]
                high = prod.astype(BF16)
                PH[g * part : (g + 1) * part, :] = high
                PL[g * part : (g + 1) * part, :] = (prod - high.astype(F32)).astype(BF16)
            score = matmul(PH[...], hmask[...]) + matmul(PL[...], hmask[...])
            pieces = [score[g * part : (g + 1) * part] for g in range(nsh)]
            top = functools.reduce(jnp.maximum, pieces)
            pieces = [jnp.exp(p - top) for p in pieces]
            scale = 1.0 / functools.reduce(jnp.add, pieces)
            mixed = jnp.zeros((part, chans), F32)
            for g in range(nsh):
                weight = matmul((pieces[g] * scale).astype(BF16), hmask_t[...])
                mixed = mixed + weight * V[g * part : (g + 1) * part, :]
            OB[pl.ds(pl.multiple_of(f * part, 16), part), :] = mixed.astype(BF16)
            return c
        lax.fori_loop(0, nsh, frame, 0)

        S2[...] = (matmul(OB[...], ao[...]) + stream[...].reshape(tokens, chans).astype(F32)).astype(BF16)
        normalise(lambda s: S2[s, :].astype(F32))
        wide = 256
        for j in range(inner // wide):
            value = matmul(N[...], gi[:, j * wide : (j + 1) * wide])
            gate = matmul(N[...], gi[:, inner + j * wide : inner + (j + 1) * wide])
            gelu = 0.5 * gate * (1.0 + lax.erf(gate * (0.5 ** 0.5)))
            ACT[:, j * wide : (j + 1) * wide] = (value * gelu).astype(BF16)
        O[n] = (matmul(ACT[...], go[...]) + S2[...].astype(F32)).astype(BF16).reshape(nsh, part, chans)

        last = n == STEPS - 1
        landing = pl.ds(pl.multiple_of(me * part, 16), part)
        target = out if last else F.at[n + 1]
        copies = []
        for d in range(nsh):
            to = lax.rem(me + d, nsh)
            if d == 0 and (last or nsec == 1):
                copies.append(pltpu.make_async_copy(O.at[n, me], target.at[landing], own_sem.at[n]))
            else:
                copies.append(pltpu.make_async_remote_copy(
                    src_ref=O.at[n, to], dst_ref=target.at[landing],
                    send_sem=out_send.at[n, d], recv_sem=out_recv.at[n, d],
                    device_id=at(to, sec if last else nxt), device_id_type=MESH,
                ))
            copies[-1].start()
        for c in copies:
            c.wait()


def solution(mesh):
    nsh, nsec = mesh.shape["shard"], mesh.shape["section"]

    def per_device(features, timesteps, conv_first, conv_second, time_weight, qkv_weight,
                   attn_out, geglu_in, geglu_out):
        _, _, rows, width, chans = features.shape
        inner = geglu_out.shape[1]
        tokens = rows * width
        part = tokens // nsh
        rim = (rows + 2) * width
        dims = (rows, width, chans, inner, nsh, nsec)
        any_ = pl.BlockSpec(memory_space=pl.ANY)
        V = pltpu.VMEM
        D = pltpu.SemaphoreType.DMA
        scratch = [
            V((STEPS, tokens, chans), BF16),
            V((STEPS, tokens, chans), F32),
            V((rim + 2 * PAD, chans), F32),
            V((rim, 3 * chans), BF16),
            V((STEPS, nsh, part, chans), BF16),
            V((STEPS, nsh, part, chans), BF16),
            V((STEPS, nsh, part, chans), BF16),
            V((2 * STEPS, 8, chans), F32),
            V((2 * STEPS, 8, chans), F32),
            V((STEPS, width, chans), BF16),
            V((STEPS, width, chans), F32),
            V((STEPS, 16, chans), F32),
            V((chans, chans), F32),
            V((chans, 128), BF16),
            V((128, chans), BF16),
            V((tokens, chans), BF16),
            V((tokens, chans), F32), V((tokens, chans), F32), V((tokens, chans), F32),
            V((tokens, chans), BF16), V((tokens, chans), BF16),
            V((tokens, chans), BF16), V((tokens, chans), BF16), V((tokens, inner), BF16),
            V((3, 3 * chans, chans), BF16), V((3, 3 * chans, chans), BF16),
            V((chans, chans), BF16), V((chans, 3 * chans), BF16), V((chans, chans), BF16),
            V((chans, 2 * inner), BF16), V((inner, chans), BF16),
            D((7,)), D((2,)), D((2 * STEPS, 2)), D((2 * STEPS, 2)),
            D((STEPS, nsh)), D((STEPS, nsh)), D((STEPS, nsh)), D((STEPS, nsh)), D((STEPS,)),
        ]
        result = pl.pallas_call(
            functools.partial(kernel, dims),
            out_shape=jax.ShapeDtypeStruct((tokens, chans), BF16),
            in_specs=[pl.BlockSpec(memory_space=pltpu.SMEM)] + [any_] * 8,
            out_specs=any_,
            scratch_shapes=scratch,
            compiler_params=pltpu.CompilerParams(
                collective_id=0, has_side_effects=True, vmem_limit_bytes=60 * 1024 * 1024
            ),
        )(
            timesteps,
            features.reshape(tokens, chans),
            conv_first.reshape(3, 3 * chans, chans),
            conv_second.reshape(3, 3 * chans, chans),
            time_weight[0], qkv_weight[0], attn_out[0], geglu_in[0], geglu_out[0],
        )
        return result.reshape(features.shape)

    return jax.shard_map(
        per_device,
        mesh=mesh,
        in_specs=(
            P(("groups", "section"), "shard", "halo", None, None),
            P(("groups", "section"), None),
            P("section", None, None, None, None),
            P("section", None, None, None, None),
            P("section", None, None),
            P("section", None, None),
            P("section", None, None),
            P("section", None, None),
            P("section", None, None),
        ),
        out_specs=P(("groups", "section"), "shard", "halo", None, None),
        check_vma=False,
    )
```

profile of v0, /device:TPU:0, one launch (start us, length us, event | category | flops | bytes accessed | tf_op | source)
XLA Modules:
  0.0 96.1 jit_solution(5584606637755184477)
XLA Ops:
  0.0 2.2 %copy.10 = bf16[1,1280,320]{2,1,0:T(8,128)(2,1)} copy(bf16[1,1280,320]{1,2,0:T(8,128)(2,1)} %param.17) | data formatting | bytes 1638400 | tf_op args[8]
  2.2 92.1 %shard_map.91 = bf16[512,320]{1,0:T(8,128)(2,1)} custom-call(s32[1,2]{1,0:T(1,128)} %stamps.1, bf16[512,320]{1,0:T(8,128)(2,1)} %bitcast.15, bf16[3,960,320]{2,1,0:T(8,128)(2,1)} %bitcast.10, bf16[3,960,320]{2,1,0:T(8,128)(2,1)} %bitcast.11, bf16[320,320]{1,0:T(8,128)(2,1)} %bitcast.16, bf16[320,960]{1,0:T(8,128)(2,1)} %bitcast.14, ...), custom_call_target="tpu_custom_call" | custom-call | tf_op jit(solution)/shard_map/pallas_call | solution.py:321
  94.3 1.8 %copy.12 = bf16[1,1,8,64,320]{4,3,2,1,0:T(8,128)(2,1)} copy(bf16[1,1,8,64,320]{4,3,2,1,0:T(8,128)(2,1)} %bitcast.13) | data formatting | bytes 655360
where the time goes:
time: 96.3 us; the launch traced here: 96.1 us
  Pallas kernels  92.1 us (96%)
  local copies, waits for them, and re-layouts  4 us (4%)
    pallas_call x1, Pallas kernels, per_device(): pl.pallas_call(functools.partial(kernel, dims), out_shape=jax.ShapeDtypeS...  92.1 us
    unnamed x2, local copies, waits for them, and re-layouts  4 us

commit v1 on v0

--- a/solution.py
+++ b/solution.py
@@ -15,6 +15,8 @@
 F32 = jnp.float32
 BF16 = jnp.bfloat16
 BLK = 64
+SUBS = 2
+UNROLL = 4
 PAD = 8
 
 
@@ -27,13 +29,15 @@
 
 
 def kernel(dims, stamps, feat, cf_h, cs_h, tw_h, qkv_h, ao_h, gi_h, go_h, out, *scratch):
-    (rows, width, chans, inner, nsh, nsec) = dims
+    (rows, width, chans, inner, nsh, nsec, subs) = dims
     (F, H, G, A, S, PB, O, stat_tx, stat_rx, edge_x, edge_h, emb, gmask, hmask, hmask_t,
      N, Q, K, V, PH, PL, OB, S2, ACT,
      cf, cs, tw, qkv, ao, gi, go,
      w_sem, x_sem, halo_send, halo_recv, in_send, in_recv, out_send, out_recv, own_sem) = scratch
     tokens = rows * width
     part = tokens // nsh
+    sub = part // subs
+    crowd = nsh * sub
     rim = (rows + 2) * width
     me = lax.axis_index("shard")
     sec = lax.axis_index("section")
@@ -120,7 +124,7 @@
             return (s1 + jnp.sum(v.reshape(BLK // 8, 8, chans), axis=0),
                     s2 + jnp.sum((v * v).reshape(BLK // 8, 8, chans), axis=0))
         z = jnp.zeros((8, chans), F32)
-        s1, s2 = lax.fori_loop(0, tokens // BLK, one, (z, z))
+        s1, s2 = lax.fori_loop(0, tokens // BLK, one, (z, z), unroll=UNROLL)
         stat_tx[slot, 0:1, :] = jnp.sum(s1, axis=0, keepdims=True)
         stat_tx[slot, 1:2, :] = jnp.sum(s2, axis=0, keepdims=True)
 
@@ -138,7 +142,7 @@
             at_ = pl.multiple_of(i * BLK, BLK)
             G[pl.ds(PAD + width + at_, BLK), :] = silu((load(pl.ds(at_, BLK)) - average) * inverse)
             return c
-        lax.fori_loop(0, tokens // BLK, one, 0)
+        lax.fori_loop(0, tokens // BLK, one, 0, unroll=UNROLL)
         G[pl.ds(rim_at, width), :] = silu((load_edge() - average) * inverse)
         col = lax.rem(lax.broadcasted_iota(jnp.int32, (width, chans), 0), width)
 
@@ -153,7 +157,7 @@
             A[dst, chans : 2 * chans] = mid.astype(BF16)
             A[dst, 2 * chans :] = jnp.where(col == width - 1, 0.0, right).astype(BF16)
             return c
-        lax.fori_loop(0, rows + 2, two, 0)
+        lax.fori_loop(0, rows + 2, two, 0, unroll=5)
 
     def conv(weights):
         total = matmul(A[pl.ds(0, tokens), :], weights[0])
@@ -169,7 +173,71 @@
             spread = jnp.mean(centred * centred, axis=-1, keepdims=True)
             N[at_, :] = (centred * lax.rsqrt(spread + 1e-05)).astype(BF16)
             return c
-        lax.fori_loop(0, tokens // BLK, one, 0)
+        lax.fori_loop(0, crowd // BLK, one, 0, unroll=UNROLL)
+
+    def gather_copy(n, k, d):
+        to = lax.rem(me + d, nsh)
+        return pltpu.make_async_remote_copy(
+            src_ref=S.at[n, k, to], dst_ref=PB.at[n, k, me],
+            send_sem=in_send.at[n, k, d], recv_sem=in_recv.at[n, k, d],
+            device_id={"shard": to}, device_id_type=MESH,
+        )
+
+    def return_copy(n, k, d):
+        last = n == STEPS - 1
+        target = out if last else F.at[n + 1]
+        landing = target.at[pl.ds(pl.multiple_of(me * part + k * sub, 16), sub)]
+        to = lax.rem(me + d, nsh)
+        if d == 0 and (last or nsec == 1):
+            return pltpu.make_async_copy(O.at[n, k, me], landing, own_sem.at[n, k])
+        return pltpu.make_async_remote_copy(
+            src_ref=O.at[n, k, to], dst_ref=landing,
+            send_sem=out_send.at[n, k, d], recv_sem=out_recv.at[n, k, d],
+            device_id=at(to, sec if last else nxt), device_id_type=MESH,
+        )
+
+    def pixels(n, k):
+        stream = PB.at[n, k]
+
+        def load_p(s):
+            return stream.reshape(crowd, chans)[s, :].astype(F32)
+        normalise(load_p)
+        proj = matmul(N[...], qkv[...]).astype(BF16)
+        Q[...] = proj[:, :chans].astype(F32)
+        K[...] = proj[:, chans : 2 * chans].astype(F32)
+        V[...] = proj[:, 2 * chans :].astype(F32)
+
+        def frame(f, c):
+            q = Q[pl.ds(pl.multiple_of(f * sub, 16), sub), :]
+            start = pl.multiple_of(f * crowd, 16)
+            for g in range(nsh):
+                prod = q * K[g * sub : (g + 1) * sub, :]
+                high = prod.astype(BF16)
+                PH[pl.ds(start + g * sub, sub), :] = high
+                PL[pl.ds(start + g * sub, sub), :] = (prod - high.astype(F32)).astype(BF16)
+            score = matmul(PH[pl.ds(start, crowd), :], hmask[...]) + matmul(PL[pl.ds(start, crowd), :], hmask[...])
+            pieces = [score[g * sub : (g + 1) * sub] for g in range(nsh)]
+            top = functools.reduce(jnp.maximum, pieces)
+            pieces = [jnp.exp(p - top) for p in pieces]
+            scale = 1.0 / functools.reduce(jnp.add, pieces)
+            weights = jnp.concatenate([(p * scale).astype(BF16) for p in pieces], axis=0)
+            weights = matmul(weights, hmask_t[...])
+            mixed = weights[0:sub] * V[0:sub, :]
+            for g in range(1, nsh):
+                mixed = mixed + weights[g * sub : (g + 1) * sub] * V[g * sub : (g + 1) * sub, :]
+            OB[pl.ds(pl.multiple_of(f * sub, 16), sub), :] = mixed.astype(BF16)
+            return c
+        lax.fori_loop(0, nsh, frame, 0, unroll=4)
+
+        S2[...] = (matmul(OB[...], ao[...]) + stream[...].reshape(crowd, chans).astype(F32)).astype(BF16)
+        normalise(lambda s: S2[s, :].astype(F32))
+        wide = 256
+        for j in range(inner // wide):
+            value = matmul(N[...], gi[:, j * wide : (j + 1) * wide])
+            gate = matmul(N[...], gi[:, inner + j * wide : inner + (j + 1) * wide])
+            gelu = 0.5 * gate * (1.0 + lax.erf(gate * (0.5 ** 0.5)))
+            ACT[:, j * wide : (j + 1) * wide] = (value * gelu).astype(BF16)
+        O[n, k] = (matmul(ACT[...], go[...]) + S2[...].astype(F32)).astype(BF16).reshape(nsh, sub, chans)
 
     for n in range(STEPS):
         if n == 0:
@@ -201,81 +269,38 @@
         activate(load_h, lambda: edge_h[n], 2 * n + 1)
         if n == 0:
             loads[1].wait()
-        S[n] = (conv(cs) + field[...].astype(F32)).astype(BF16).reshape(nsh, part, chans)
-
-        copies = []
-        for d in range(1, nsh):
-            to = lax.rem(me + d, nsh)
-            copies.append(pltpu.make_async_remote_copy(
-                src_ref=S.at[n, to], dst_ref=PB.at[n, me],
-                send_sem=in_send.at[n, d], recv_sem=in_recv.at[n, d],
-                device_id={"shard": to}, device_id_type=MESH,
-            ))
-            copies[-1].start()
-        PB[n, me] = S[n, me]
-        for c in copies:
-            c.wait()
+        for k in range(subs):
+            spans = [j * part + k * sub for j in range(nsh)]
+            total = sum(
+                matmul(jnp.concatenate([A[pl.ds(r * width + a, sub), :] for a in spans], axis=0), cs[r])
+                for r in range(3)
+            )
+            base = jnp.concatenate([field[pl.ds(a, sub), :] for a in spans], axis=0)
+            S[n, k] = (total + base.astype(F32)).astype(BF16).reshape(nsh, sub, chans)
+            for d in range(1, nsh):
+                gather_copy(n, k, d).start()
+            PB[n, k, me] = S[n, k, me]
 
         if n == 0:
             for i in (3, 4, 5, 6):
                 loads[i].wait()
-        stream = PB.at[n]
-
-        def load_p(s):
-            return stream.reshape(tokens, chans)[s, :].astype(F32)
-        normalise(load_p)
-        proj = matmul(N[...], qkv[...]).astype(BF16)
-        Q[...] = proj[:, :chans].astype(F32)
-        K[...] = proj[:, chans : 2 * chans].astype(F32)
-        V[...] = proj[:, 2 * chans :].astype(F32)
-
-        def frame(f, c):
-            q = Q[pl.ds(pl.multiple_of(f * part, 16), part), :]
-            for g in range(nsh):
-                prod = q * K[g * part : (g + 1) * part, :]
-                high = prod.astype(BF16)
-                PH[g * part : (g + 1) * part, :] = high
-                PL[g * part : (g + 1) * part, :] = (prod - high.astype(F32)).astype(BF16)
-            score = matmul(PH[...], hmask[...]) + matmul(PL[...], hmask[...])
-            pieces = [score[g * part : (g + 1) * part] for g in range(nsh)]
-            top = functools.reduce(jnp.maximum, pieces)
-            pieces = [jnp.exp(p - top) for p in pieces]
-            scale = 1.0 / functools.reduce(jnp.add, pieces)
-            mixed = jnp.zeros((part, chans), F32)
-            for g in range(nsh):
-                weight = matmul((pieces[g] * scale).astype(BF16), hmask_t[...])
-                mixed = mixed + weight * V[g * part : (g + 1) * part, :]
-            OB[pl.ds(pl.multiple_of(f * part, 16), part), :] = mixed.astype(BF16)
-            return c
-        lax.fori_loop(0, nsh, frame, 0)
-
-        S2[...] = (matmul(OB[...], ao[...]) + stream[...].reshape(tokens, chans).astype(F32)).astype(BF16)
-        normalise(lambda s: S2[s, :].astype(F32))
-        wide = 256
-        for j in range(inner // wide):
-            value = matmul(N[...], gi[:, j * wide : (j + 1) * wide])
-            gate = matmul(N[...], gi[:, inner + j * wide : inner + (j + 1) * wide])
-            gelu = 0.5 * gate * (1.0 + lax.erf(gate * (0.5 ** 0.5)))
-            ACT[:, j * wide : (j + 1) * wide] = (value * gelu).astype(BF16)
-        O[n] = (matmul(ACT[...], go[...]) + S2[...].astype(F32)).astype(BF16).reshape(nsh, part, chans)
-
-        last = n == STEPS - 1
-        landing = pl.ds(pl.multiple_of(me * part, 16), part)
-        target = out if last else F.at[n + 1]
-        copies = []
-        for d in range(nsh):
-            to = lax.rem(me + d, nsh)
-            if d == 0 and (last or nsec == 1):
-                copies.append(pltpu.make_async_copy(O.at[n, me], target.at[landing], own_sem.at[n]))
-            else:
-                copies.append(pltpu.make_async_remote_copy(
-                    src_ref=O.at[n, to], dst_ref=target.at[landing],
-                    send_sem=out_send.at[n, d], recv_sem=out_recv.at[n, d],
-                    device_id=at(to, sec if last else nxt), device_id_type=MESH,
-                ))
-            copies[-1].start()
-        for c in copies:
-            c.wait()
+
+        def temporal(k, carry, n=n):
+            for d in range(1, nsh):
+                gather_copy(n, k, d).wait_recv()
+            pixels(n, k)
+            for d in range(nsh):
+                return_copy(n, k, d).start()
+            return carry
+        lax.fori_loop(0, subs, temporal, 0)
+
+        def settle(k, carry, n=n):
+            for d in range(1, nsh):
+                gather_copy(n, k, d).wait_send()
+            for d in range(nsh):
+                return_copy(n, k, d).wait()
+            return carry
+        lax.fori_loop(0, subs, settle, 0)
 
 
 def solution(mesh):
@@ -288,7 +313,10 @@
         tokens = rows * width
         part = tokens // nsh
         rim = (rows + 2) * width
-        dims = (rows, width, chans, inner, nsh, nsec)
+        subs = min(SUBS, part // 16)
+        dims = (rows, width, chans, inner, nsh, nsec, subs)
+        sub = part // subs
+        crowd = nsh * sub
         any_ = pl.BlockSpec(memory_space=pl.ANY)
         V = pltpu.VMEM
         D = pltpu.SemaphoreType.DMA
@@ -297,9 +325,9 @@
             V((STEPS, tokens, chans), F32),
             V((rim + 2 * PAD, chans), F32),
             V((rim, 3 * chans), BF16),
-            V((STEPS, nsh, part, chans), BF16),
-            V((STEPS, nsh, part, chans), BF16),
-            V((STEPS, nsh, part, chans), BF16),
+            V((STEPS, subs, nsh, sub, chans), BF16),
+            V((STEPS, subs, nsh, sub, chans), BF16),
+            V((STEPS, subs, nsh, sub, chans), BF16),
             V((2 * STEPS, 8, chans), F32),
             V((2 * STEPS, 8, chans), F32),
             V((STEPS, width, chans), BF16),
@@ -308,15 +336,16 @@
             V((chans, chans), F32),
             V((chans, 128), BF16),
             V((128, chans), BF16),
-            V((tokens, chans), BF16),
-            V((tokens, chans), F32), V((tokens, chans), F32), V((tokens, chans), F32),
-            V((tokens, chans), BF16), V((tokens, chans), BF16),
-            V((tokens, chans), BF16), V((tokens, chans), BF16), V((tokens, inner), BF16),
+            V((crowd, chans), BF16),
+            V((crowd, chans), F32), V((crowd, chans), F32), V((crowd, chans), F32),
+            V((nsh * crowd, chans), BF16), V((nsh * crowd, chans), BF16),
+            V((crowd, chans), BF16), V((crowd, chans), BF16), V((crowd, inner), BF16),
             V((3, 3 * chans, chans), BF16), V((3, 3 * chans, chans), BF16),
             V((chans, chans), BF16), V((chans, 3 * chans), BF16), V((chans, chans), BF16),
             V((chans, 2 * inner), BF16), V((inner, chans), BF16),
             D((7,)), D((2,)), D((2 * STEPS, 2)), D((2 * STEPS, 2)),
-            D((STEPS, nsh)), D((STEPS, nsh)), D((STEPS, nsh)), D((STEPS, nsh)), D((STEPS,)),
+            D((STEPS, subs, nsh)), D((STEPS, subs, nsh)), D((STEPS, subs, nsh)), D((STEPS, subs, nsh)),
+            D((STEPS, subs)),
         ]
         result = pl.pallas_call(
             functools.partial(kernel, dims),

time: 96.3 us -> 77.5 us (0.80)
  Pallas kernels: 92.1 us -> 73.3 us
    pallas_call x1, Pallas kernels: 92.1 us -> 73.3 us  [per_device(): pl.pallas_call(functools.partial(kernel, dims), out_shape=jax.ShapeDtypeS...]
where the time goes in v1:
time: 77.5 us; the launch traced here: 77.3 us
  Pallas kernels  73.3 us (95%)
  local copies, waits for them, and re-layouts  4 us (5%)
    pallas_call x1, Pallas kernels, per_device(): pl.pallas_call(functools.partial(kernel, dims), out_shape=jax.ShapeDtypeS...  73.3 us
    unnamed x2, local copies, waits for them, and re-layouts  4 us

profile of v1, /device:TPU:0, one launch (start us, length us, event | category | flops | bytes accessed | tf_op | source)
XLA Modules:
  0.0 77.3 jit_solution(16663547999752940882)
XLA Ops:
  0.0 2.2 %copy.10 = bf16[1,1280,320]{2,1,0:T(8,128)(2,1)} copy(bf16[1,1280,320]{1,2,0:T(8,128)(2,1)} %param.17) | data formatting | bytes 1638400 | tf_op args[8]
  2.2 73.3 %shard_map.91 = bf16[512,320]{1,0:T(8,128)(2,1)} custom-call(s32[1,2]{1,0:T(1,128)} %stamps.1, bf16[512,320]{1,0:T(8,128)(2,1)} %bitcast.15, bf16[3,960,320]{2,1,0:T(8,128)(2,1)} %bitcast.10, bf16[3,960,320]{2,1,0:T(8,128)(2,1)} %bitcast.11, bf16[320,320]{1,0:T(8,128)(2,1)} %bitcast.16, bf16[320,960]{1,0:T(8,128)(2,1)} %bitcast.14, ...), custom_call_target="tpu_custom_call" | custom-call | tf_op jit(solution)/shard_map/pallas_call | solution.py:350
  75.5 1.8 %copy.12 = bf16[1,1,8,64,320]{4,3,2,1,0:T(8,128)(2,1)} copy(bf16[1,1,8,64,320]{4,3,2,1,0:T(8,128)(2,1)} %bitcast.13) | data formatting | bytes 655360

commit v2 on v1

--- a/solution.py
+++ b/solution.py
@@ -17,6 +17,7 @@
 BLK = 64
 SUBS = 2
 UNROLL = 4
+SHIFTS = 4
 PAD = 8
 
 
@@ -30,10 +31,10 @@
 
 def kernel(dims, stamps, feat, cf_h, cs_h, tw_h, qkv_h, ao_h, gi_h, go_h, out, *scratch):
     (rows, width, chans, inner, nsh, nsec, subs) = dims
-    (F, H, G, A, S, PB, O, stat_tx, stat_rx, edge_x, edge_h, emb, gmask, hmask, hmask_t,
+    (F, FX, first_rx, H, G, A, S, PB, O, stat_tx, stat_rx, edge_x, edge_h, emb, gmask, hmask, hmask_t,
      N, Q, K, V, PH, PL, OB, S2, ACT,
      cf, cs, tw, qkv, ao, gi, go,
-     w_sem, x_sem, halo_send, halo_recv, in_send, in_recv, out_send, out_recv, own_sem) = scratch
+     w_sem, x_send, x_recv, first_send, first_recv, halo_send, halo_recv, in_send, in_recv, out_send, out_recv, own_sem) = scratch
     tokens = rows * width
     part = tokens // nsh
     sub = part // subs
@@ -44,6 +45,8 @@
     side = lax.axis_index("halo")
     nxt = lax.rem(sec + 1, nsec)
 
+    own = pltpu.make_async_copy(feat, FX, w_sem.at[7])
+    own.start()
     loads = [
         pltpu.make_async_copy(src, dst, w_sem.at[i])
         for i, (src, dst) in enumerate(
@@ -63,15 +66,57 @@
     for e in sorted({1 % nsec, (nsec - 1) % nsec} - {0}):
         for d in range(nsh):
             peers.append(at(lax.rem(me + d, nsh), lax.rem(sec + e, nsec)))
+        peers.append({"section": lax.rem(sec + e, nsec), "halo": 1 - side})
     for peer in peers:
         pl.semaphore_signal(barrier, inc=1, device_id=peer, device_id_type=MESH)
     pl.semaphore_wait(barrier, len(peers))
 
-    shift = pltpu.make_async_remote_copy(
-        src_ref=feat, dst_ref=F.at[0], send_sem=x_sem.at[0], recv_sem=x_sem.at[1],
-        device_id={"section": nxt}, device_id_type=MESH,
-    )
-    shift.start()
+    edge_at = pl.multiple_of((1 - side) * (tokens - width), 16)
+    piece = tokens // SHIFTS
+    shifts = [
+        pltpu.make_async_remote_copy(
+            src_ref=feat.at[pl.ds(i * piece, piece)], dst_ref=F.at[0, pl.ds(i * piece, piece)],
+            send_sem=x_send.at[i], recv_sem=x_recv.at[i],
+            device_id={"section": nxt}, device_id_type=MESH,
+        )
+        for i in range(SHIFTS)
+    ]
+    firsts = [
+        pltpu.make_async_remote_copy(
+            src_ref=src, dst_ref=dst, send_sem=first_send.at[i], recv_sem=first_recv.at[i],
+            device_id={"section": nxt, "halo": core}, device_id_type=MESH,
+        )
+        for i, (src, dst, core) in enumerate((
+            (stat_tx.at[0], first_rx.at[0], side),
+            (stat_tx.at[0], first_rx.at[1], 1 - side),
+            (feat.at[pl.ds(edge_at, width)], edge_x.at[0], 1 - side),
+        ))
+    ]
+    firsts[2].start()
+    for i in range(SHIFTS // 2):
+        shifts[i].start()
+    stat_tx[...] = jnp.zeros_like(stat_tx)
+
+    def fold(carry, v):
+        s1, s2 = carry
+        v = v.reshape(v.shape[0] // 8, 8, chans)
+        return s1 + jnp.sum(v, axis=0), s2 + jnp.sum(v * v, axis=0)
+
+    none = (jnp.zeros((8, chans), F32), jnp.zeros((8, chans), F32))
+
+    def publish(slot, sums):
+        stat_tx[slot, 0:1, :] = jnp.sum(sums[0], axis=0, keepdims=True)
+        stat_tx[slot, 1:2, :] = jnp.sum(sums[1], axis=0, keepdims=True)
+
+    own.wait()
+
+    def own_total(i, carry):
+        return fold(carry, FX[pl.ds(pl.multiple_of(i * BLK, BLK), BLK), :].astype(F32))
+    publish(0, lax.fori_loop(0, tokens // BLK, own_total, none, unroll=UNROLL))
+    firsts[0].start()
+    firsts[1].start()
+    for i in range(SHIFTS // 2, SHIFTS):
+        shifts[i].start()
 
     per = chans // GROUPS
     ci = lax.broadcasted_iota(jnp.int32, (chans, chans), 0)
@@ -84,7 +129,6 @@
     ti_ = lax.broadcasted_iota(jnp.int32, (lanes, chans), 0)
     tj_ = lax.broadcasted_iota(jnp.int32, (lanes, chans), 1)
     hmask_t[...] = jnp.where(tj_ - lax.rem(tj_, HEAD_DIM) == ti_ * HEAD_DIM, 1.0, 0.0).astype(BF16)
-    stat_tx[...] = jnp.zeros_like(stat_tx)
     zeros_rim = jnp.zeros((width, chans), F32)
     G[pl.ds(0, PAD), :] = jnp.zeros((PAD, chans), F32)
     G[pl.ds(PAD + rim, PAD), :] = jnp.zeros((PAD, chans), F32)
@@ -101,7 +145,6 @@
         wave = jnp.where(lane < half, jnp.cos(angles), jnp.sin(angles))
         emb[n] = matmul(silu(wave).astype(BF16), tw[...])
 
-    edge_at = pl.multiple_of((1 - side) * (tokens - width), 16)
     rim_at = pl.multiple_of(PAD + (1 - side) * (rim - width), 8)
     count = float(rows * 2 * width * per)
 
@@ -117,32 +160,24 @@
         ]
         return copies
 
-    def totals(load, slot):
-        def one(i, carry):
-            s1, s2 = carry
-            v = load(pl.ds(pl.multiple_of(i * BLK, BLK), BLK))
-            return (s1 + jnp.sum(v.reshape(BLK // 8, 8, chans), axis=0),
-                    s2 + jnp.sum((v * v).reshape(BLK // 8, 8, chans), axis=0))
-        z = jnp.zeros((8, chans), F32)
-        s1, s2 = lax.fori_loop(0, tokens // BLK, one, (z, z), unroll=UNROLL)
-        stat_tx[slot, 0:1, :] = jnp.sum(s1, axis=0, keepdims=True)
-        stat_tx[slot, 1:2, :] = jnp.sum(s2, axis=0, keepdims=True)
-
-    def moments(slot):
-        both = stat_tx[slot] + stat_rx[slot]
+    def moments(both):
         summed = jnp.dot(both, gmask[...], preferred_element_type=F32, precision=lax.Precision.HIGHEST)
         average = summed[0:1, :] / count
         second = summed[1:2, :] / count
         return average, lax.rsqrt(second - average * average + 1e-05)
 
-    def activate(load, load_edge, slot):
-        average, inverse = moments(slot)
+    def activate(load, load_edge, both, arrivals=()):
+        average, inverse = moments(both)
 
         def one(i, c):
             at_ = pl.multiple_of(i * BLK, BLK)
             G[pl.ds(PAD + width + at_, BLK), :] = silu((load(pl.ds(at_, BLK)) - average) * inverse)
             return c
-        lax.fori_loop(0, tokens // BLK, one, 0, unroll=UNROLL)
+        stages = max(len(arrivals), 1)
+        for i in range(stages):
+            if arrivals:
+                arrivals[i].wait_recv()
+            lax.fori_loop(i * (tokens // BLK) // stages, (i + 1) * (tokens // BLK) // stages, one, 0, unroll=2)
         G[pl.ds(rim_at, width), :] = silu((load_edge() - average) * inverse)
         col = lax.rem(lax.broadcasted_iota(jnp.int32, (width, chans), 0), width)
 
@@ -159,11 +194,8 @@
             return c
         lax.fori_loop(0, rows + 2, two, 0, unroll=5)
 
-    def conv(weights):
-        total = matmul(A[pl.ds(0, tokens), :], weights[0])
-        total += matmul(A[pl.ds(width, tokens), :], weights[1])
-        total += matmul(A[pl.ds(2 * width, tokens), :], weights[2])
-        return total
+    def conv(weights, start, size):
+        return sum(matmul(A[pl.ds(start + r * width, size), :], weights[r]) for r in range(3))
 
     def normalise(src):
         def one(i, c):
@@ -240,33 +272,41 @@
         O[n, k] = (matmul(ACT[...], go[...]) + S2[...].astype(F32)).astype(BF16).reshape(nsh, sub, chans)
 
     for n in range(STEPS):
-        if n == 0:
-            shift.wait()
         field = F.at[n]
 
         def load_x(s, field=field):
             return field[s, :].astype(F32)
 
-        swaps = swap(2 * n, field.at[pl.ds(edge_at, width)], edge_x.at[n])
+        if n == 0:
+            for c in firsts:
+                c.wait()
+            activate(load_x, lambda: edge_x[0].astype(F32), first_rx[0] + first_rx[1], shifts)
+            for c in shifts:
+                c.wait_send()
+            loads[0].wait()
+        else:
+            swaps = swap(2 * n, field.at[pl.ds(edge_at, width)], edge_x.at[n])
+            swaps[0].start()
+            publish(2 * n, sums)
+            swaps[1].start()
+            for c in swaps:
+                c.wait()
+            activate(load_x, lambda n=n: edge_x[n].astype(F32), stat_tx[2 * n] + stat_rx[2 * n])
+        sums = none
+        for i in range(2):
+            rows_ = pl.ds(i * (tokens // 2), tokens // 2)
+            h1 = conv(cf, i * (tokens // 2), tokens // 2) + emb[n, 0:1, :]
+            H[n, rows_, :] = h1
+            sums = fold(sums, h1)
+
+        slot = 2 * n + 1
+        swaps = swap(slot, H.at[n, pl.ds(edge_at, width)], edge_h.at[n])
         swaps[0].start()
-        totals(load_x, 2 * n)
+        publish(slot, sums)
         swaps[1].start()
-        for s in swaps:
-            s.wait()
-        activate(load_x, lambda: edge_x[n].astype(F32), 2 * n)
-        if n == 0:
-            loads[0].wait()
-        H[n] = conv(cf) + emb[n, 0:1, :]
-
-        def load_h(s):
-            return H[n, s, :]
-        swaps = swap(2 * n + 1, H.at[n, pl.ds(edge_at, width)], edge_h.at[n])
-        swaps[0].start()
-        totals(load_h, 2 * n + 1)
-        swaps[1].start()
-        for s in swaps:
-            s.wait()
-        activate(load_h, lambda: edge_h[n], 2 * n + 1)
+        for c in swaps:
+            c.wait()
+        activate(lambda s, n=n: H[n, s, :], lambda n=n: edge_h[n], stat_tx[slot] + stat_rx[slot])
         if n == 0:
             loads[1].wait()
         for k in range(subs):
@@ -294,13 +334,16 @@
             return carry
         lax.fori_loop(0, subs, temporal, 0)
 
-        def settle(k, carry, n=n):
+        sums = none
+        for k in range(subs):
+            for d in range(nsh):
+                return_copy(n, k, d).wait()
+            if n < STEPS - 1:
+                for j in range(nsh):
+                    sums = fold(sums, F[n + 1, pl.ds(j * part + k * sub, sub), :].astype(F32))
+        for k in range(subs):
             for d in range(1, nsh):
                 gather_copy(n, k, d).wait_send()
-            for d in range(nsh):
-                return_copy(n, k, d).wait()
-            return carry
-        lax.fori_loop(0, subs, settle, 0)
 
 
 def solution(mesh):
@@ -322,6 +365,8 @@
         D = pltpu.SemaphoreType.DMA
         scratch = [
             V((STEPS, tokens, chans), BF16),
+            V((tokens, chans), BF16),
+            V((2, 8, chans), F32),
             V((STEPS, tokens, chans), F32),
             V((rim + 2 * PAD, chans), F32),
             V((rim, 3 * chans), BF16),
@@ -343,7 +388,7 @@
             V((3, 3 * chans, chans), BF16), V((3, 3 * chans, chans), BF16),
             V((chans, chans), BF16), V((chans, 3 * chans), BF16), V((chans, chans), BF16),
             V((chans, 2 * inner), BF16), V((inner, chans), BF16),
-            D((7,)), D((2,)), D((2 * STEPS, 2)), D((2 * STEPS, 2)),
+            D((8,)), D((SHIFTS,)), D((SHIFTS,)), D((3,)), D((3,)), D((2 * STEPS, 2)), D((2 * STEPS, 2)),
             D((STEPS, subs, nsh)), D((STEPS, subs, nsh)), D((STEPS, subs, nsh)), D((STEPS, subs, nsh)),
             D((STEPS, subs)),
         ]

time: 77.5 us -> 76.1 us (0.982)
  Pallas kernels: 73.3 us -> 71.9 us
    pallas_call x1, Pallas kernels: 73.3 us -> 71.9 us  [per_device(): pl.pallas_call(functools.partial(kernel, dims), out_shape=jax.ShapeDtypeS...]
where the time goes in v2:
time: 76.1 us; the launch traced here: 75.9 us
  Pallas kernels  71.9 us (94%)
  local copies, waits for them, and re-layouts  4 us (5%)
    pallas_call x1, Pallas kernels, per_device(): pl.pallas_call(functools.partial(kernel, dims), out_shape=jax.ShapeDtypeS...  71.9 us
    unnamed x2, local copies, waits for them, and re-layouts  4 us

profile of v2, /device:TPU:0, one launch (start us, length us, event | category | flops | bytes accessed | tf_op | source)
XLA Modules:
  0.0 75.9 jit_solution(16969688864111240694)
XLA Ops:
  0.0 2.2 %copy.10 = bf16[1,1280,320]{2,1,0:T(8,128)(2,1)} copy(bf16[1,1280,320]{1,2,0:T(8,128)(2,1)} %param.17) | data formatting | bytes 1638400 | tf_op args[8]
  2.2 71.9 %shard_map.91 = bf16[512,320]{1,0:T(8,128)(2,1)} custom-call(s32[1,2]{1,0:T(1,128)} %stamps.1, bf16[512,320]{1,0:T(8,128)(2,1)} %bitcast.15, bf16[3,960,320]{2,1,0:T(8,128)(2,1)} %bitcast.10, bf16[3,960,320]{2,1,0:T(8,128)(2,1)} %bitcast.11, bf16[320,320]{1,0:T(8,128)(2,1)} %bitcast.16, bf16[320,960]{1,0:T(8,128)(2,1)} %bitcast.14, ...), custom_call_target="tpu_custom_call" | custom-call | tf_op jit(solution)/shard_map/pallas_call | solution.py:395
  74.2 1.8 %copy.12 = bf16[1,1,8,64,320]{4,3,2,1,0:T(8,128)(2,1)} copy(bf16[1,1,8,64,320]{4,3,2,1,0:T(8,128)(2,1)} %bitcast.13) | data formatting | bytes 655360

commit v3 on v2

--- a/solution.py
+++ b/solution.py
@@ -23,6 +23,10 @@
 
 def matmul(a, b):
     return jnp.dot(a, b, preferred_element_type=F32)
+
+
+def matmul_t(a, b):
+    return lax.dot_general(a, b, (((1,), (1,)), ((), ())), preferred_element_type=F32)
 
 
 def silu(u):
@@ -269,7 +273,7 @@
             gate = matmul(N[...], gi[:, inner + j * wide : inner + (j + 1) * wide])
             gelu = 0.5 * gate * (1.0 + lax.erf(gate * (0.5 ** 0.5)))
             ACT[:, j * wide : (j + 1) * wide] = (value * gelu).astype(BF16)
-        O[n, k] = (matmul(ACT[...], go[...]) + S2[...].astype(F32)).astype(BF16).reshape(nsh, sub, chans)
+        O[n, k] = (matmul_t(ACT[...], go[...]) + S2[...].astype(F32)).astype(BF16).reshape(nsh, sub, chans)
 
     for n in range(STEPS):
         field = F.at[n]
@@ -387,7 +391,7 @@
             V((crowd, chans), BF16), V((crowd, chans), BF16), V((crowd, inner), BF16),
             V((3, 3 * chans, chans), BF16), V((3, 3 * chans, chans), BF16),
             V((chans, chans), BF16), V((chans, 3 * chans), BF16), V((chans, chans), BF16),
-            V((chans, 2 * inner), BF16), V((inner, chans), BF16),
+            V((chans, 2 * inner), BF16), V((chans, inner), BF16),
             D((8,)), D((SHIFTS,)), D((SHIFTS,)), D((3,)), D((3,)), D((2 * STEPS, 2)), D((2 * STEPS, 2)),
             D((STEPS, subs, nsh)), D((STEPS, subs, nsh)), D((STEPS, subs, nsh)), D((STEPS, subs, nsh)),
             D((STEPS, subs)),
@@ -406,7 +410,7 @@
             features.reshape(tokens, chans),
             conv_first.reshape(3, 3 * chans, chans),
             conv_second.reshape(3, 3 * chans, chans),
-            time_weight[0], qkv_weight[0], attn_out[0], geglu_in[0], geglu_out[0],
+            time_weight[0], qkv_weight[0], attn_out[0], geglu_in[0], jnp.swapaxes(geglu_out[0], 0, 1),
         )
         return result.reshape(features.shape)
 

time: 76.1 us -> 73.9 us (0.971)
  local copies, waits for them, and re-layouts: 4 us -> 1.78 us
    unnamed x2 -> x1, local copies, waits for them, and re-layouts: 4 us -> 1.78 us
where the time goes in v3:
time: 73.9 us; the launch traced here: 73.7 us
  Pallas kernels  71.9 us (97%)
  local copies, waits for them, and re-layouts  1.78 us (2%)
    pallas_call x1, Pallas kernels, per_device(): pl.pallas_call(functools.partial(kernel, dims), out_shape=jax.ShapeDtypeS...  71.9 us
    unnamed x1, local copies, waits for them, and re-layouts  1.78 us

profile of v3, /device:TPU:0, one launch (start us, length us, event | category | flops | bytes accessed | tf_op | source)
XLA Modules:
  0.0 73.7 jit_solution(12166551807475792505)
XLA Ops:
  0.0 71.9 %shard_map.91 = bf16[512,320]{1,0:T(8,128)(2,1)} custom-call(s32[1,2]{1,0:T(1,128)} %stamps.1, bf16[512,320]{1,0:T(8,128)(2,1)} %bitcast.17, bf16[3,960,320]{2,1,0:T(8,128)(2,1)} %bitcast.11, bf16[3,960,320]{2,1,0:T(8,128)(2,1)} %bitcast.12, bf16[320,320]{1,0:T(8,128)(2,1)} %bitcast.18, bf16[320,960]{1,0:T(8,128)(2,1)} %bitcast.16, ...), custom_call_target="tpu_custom_call" | custom-call | tf_op jit(solution)/shard_map/pallas_call | solution.py:399
  72.0 1.8 %copy.11 = bf16[1,1,8,64,320]{4,3,2,1,0:T(8,128)(2,1)} copy(bf16[1,1,8,64,320]{4,3,2,1,0:T(8,128)(2,1)} %bitcast.14) | data formatting | bytes 655360
